TPU v7x, 256 devices: a whole 4x4x8 slice. The times are simulated.
256 devices in a mesh: layer: 8 (over y_lo, x), feat: 32 (over z, y_hi, core).
Axes of the slice: x: 4, y: 4 (y_hi: 2, y_lo: 2; y = y_hi * 2 + y_lo), z: 8, core: 2. Of those that a mesh axis runs over, the one named last changes fastest.
Arguments:
- inputs: bfloat16 [8, 128, 2304], P('layer'), may hold values from -6 to 6
- targets: bfloat16 [8, 128, 2304], P('layer', None, 'feat'), may hold values from -6 to 6
- w_enc: bfloat16 [8, 2304, 2048], P('layer', None, 'feat'), may hold values from -0.125 to 0.125
- b_enc: float32 [8, 2048], P('layer', 'feat'), may hold values from -3 to 3
- w_dec: bfloat16 [8, 8, 2048, 2304], P('layer', None, 'feat'), may hold values from -0.046875 to 0.046875
Outputs:
- grad_enc: bfloat16 [8, 2304, 2048], P('layer', None, 'feat')
- grad_dec: bfloat16 [8, 8, 2048, 2304], P('layer', None, 'feat')
- grad_benc: float32 [8, 2048], P('layer', 'feat')
All inputs are finite; a program needn't handle non-finite values.
Results may differ from a plain program's by a relative error of at most 0.0085.
Values may be sent and summed in bfloat16 or wider, within the bound.
A program may use at most 64 MiB of HBM per device.

v0:
```python
import jax
import jax.numpy as jnp
from jax import lax
from jax.sharding import PartitionSpec as P


def shards(inputs, targets, w_enc, b_enc, w_dec):
    layer_count = w_dec.shape[1]
    feat_count = lax.axis_size("feat")
    tok_count = inputs.shape[1]
    model_width = inputs.shape[2]
    col_count = model_width // feat_count
    slab_width = w_dec.shape[2]
    grad_scale = tok_count ** (-0.5)
    own_layer = lax.axis_index("layer")
    pre_act = jnp.dot(inputs[0], w_enc[0], preferred_element_type=jnp.float32) + b_enc[0]
    active = jax.nn.relu(pre_act).astype(jnp.bfloat16)
    later_mask = jnp.arange(layer_count) >= own_layer
    later_float = later_mask.astype(jnp.float32)
    later_half = later_mask.astype(jnp.bfloat16)
    weights = w_dec[0]
    blocks = weights.reshape(layer_count, slab_width, feat_count, col_count)
    partials = jnp.einsum("tf,mfnc->mntc", active, blocks, preferred_element_type=jnp.float32)
    partials = partials * later_float[:, None, None, None]
    partials = partials.reshape(layer_count * feat_count, tok_count, col_count)
    rebuilt = lax.psum_scatter(partials, ("layer", "feat"), scatter_dimension=0, tiled=True)[0]
    errors = (rebuilt - targets[0].astype(jnp.float32)).astype(jnp.bfloat16)
    err_block = errors[None, None]
    everything = lax.all_gather(err_block, ("layer", "feat"), axis=0, tiled=True)
    everything = everything.reshape(layer_count, feat_count, tok_count, col_count)
    masked = everything * later_half[:, None, None, None]
    act_grad = grad_scale * jnp.einsum(
        "mntc,mfnc->tf", masked, blocks, preferred_element_type=jnp.float32
    )
    dec_grad = (
        jnp.einsum("tf,mntc->mfnc", active, masked, preferred_element_type=jnp.float32) * grad_scale
    )
    grad_dec = dec_grad.astype(jnp.bfloat16).reshape(layer_count, slab_width, model_width)
    pre_grad = jnp.where(pre_act > 0, act_grad, 0.0).astype(jnp.bfloat16)
    grad_enc = jnp.einsum(
        "td,tf->df", inputs[0], pre_grad, preferred_element_type=jnp.float32
    ).astype(jnp.bfloat16)
    grad_benc = jnp.sum(pre_grad.astype(jnp.float32), axis=0)
    return (grad_enc[None], grad_dec[None], grad_benc[None])


def solution(mesh):
    in_specs = (
        P("layer", None, None),
        P("layer", None, "feat"),
        P("layer", None, "feat"),
        P("layer", "feat"),
        P("layer", None, "feat", None),
    )
    out_specs = (P("layer", None, "feat"), P("layer", None, "feat", None), P("layer", "feat"))
    return jax.shard_map(shards, mesh=mesh, in_specs=in_specs, out_specs=out_specs, check_vma=False)
```

profile of v0, /device:TPU:1, one launch (start us, length us, event | category | flops | bytes accessed | tf_op | source)
XLA Modules:
  0.0 1770.6 jit_solution(4785494572840686136)
XLA Ops:
  7.2 0.0 copy-start
  7.2 0.0 copy-start.4
  7.2 0.0 copy-start.2
  7.2 0.0 reduce-scatter.5.cloned.1.call-start
  7.3 11.4 reshape_squeeze.3
  18.6 0.0 copy-done
  18.6 0.0 copy-done.4
  18.6 0.0 copy-done.2
  18.6 0.3 convolution_add_fusion
  19.0 8.7 broadcast_multiply_fusion
  27.7 0.0 copy-start.3
  27.7 0.0 reduce-scatter.5.cloned.1.call-update
  27.7 0.2 all-gather.3.cloned.1.call-start
  27.9 1293.9 %reduce-scatter.5.cloned.1.call-done = f32[1,128,72]{1,2,0:T(8,128)} async-done(((f32[256,128,72]{1,2,0:T(8,128)}), f32[1,128,72]{1,2,0:T(8,128)}) %reduce-scatter.5.cloned.1.call-update) | async-done | bytes 36880
  1321.8 0.0 copy-done.3
  1321.8 1.4 subtract_convert_fusion
  1323.2 0.0 all-gather.3.cloned.1.call-update
  1323.3 415.3 %all-gather.3.cloned.1.call-done = bf16[256,128,72]{1,2,0:T(8,128)(2,1)} async-done(((bf16[1,128,72]{1,2,0:T(8,128)(2,1)}), bf16[256,128,72]{1,2,0:T(8,128)(2,1)}) %all-gather.3.cloned.1.call-update) | async-done | bytes 4718608 | tf_op jit(solution)/shard_map/all_gather | solution.py:29
  1738.6 7.0 convert_reduce_fusion
  1745.6 0.0 copy-done.1
  1745.6 4.3 fusion
  1749.9 4.8 copy.15
  1754.7 8.1 broadcast_in_dim_reshape.3
  1762.9 0.9 fusion.10
  (3 shorter events, 0.0 us)
Async XLA Ops:
  7.2 11.5 copy-start
  7.2 11.4 copy-start.4
  7.2 11.4 copy-start.2
  7.2 1314.6 %reduce-scatter.5.cloned.1.call-start = ((), (), s32[]{:S(2)}) async-start(), calls=%async_computation.2 | async-start | bytes 9474048
  27.7 1294.2 %copy-start.3 = (bf16[1,128,72]{1,2,0:T(8,128)(2,1)S(1)}, bf16[1,128,72]{1,2,0:T(8,128)(2,1)}, u32[]{:S(2)}) copy-start(bf16[1,128,72]{1,2,0:T(8,128)(2,1)} %param.6) | copy-start | bytes 55300
  27.7 1710.9 %all-gather.3.cloned.1.call-start = ((), (), s32[]{:S(2)}) async-start(), calls=%async_computation.1 | async-start | bytes 4737024 | tf_op jit(solution)/shard_map/all_gather | solution.py:29
  1738.6 7.0 copy-start.1
Sparse Core Ops, SparseCore 0:
  27.8 1293.9 reduce-scatter.4
  1324.3 414.2 all-gather.2
where the time goes:
time: 1770 us
  waiting for transfers between devices  1710 us (97%)
  local copies, waits for them, and re-layouts  24.3 us (1%)
  matrix products  21.3 us (1%)
    unnamed x3, waiting for transfers between devices  1290 us
    all_gather x1, waiting for transfers between devices, shards(): lax.all_gather(err_block, ('layer', 'feat'), axis=0, tiled=True)  415 us
  transfers between devices with their start and end apart: 2, of which 2 were waited for; matrix products, arithmetic and copies ran while one was open for 0% of the time, Pallas kernels for 0%

commit v1 on v0

v1 whole, which is shorter than its diff:
```python
import functools

import jax
import jax.numpy as jnp
from jax import lax
from jax.experimental import pallas as pl
from jax.experimental.pallas import tpu as pltpu
from jax.sharding import PartitionSpec as P

MESH = pl.DeviceIdType.MESH
F32 = jnp.float32
BF16 = jnp.bfloat16

NX = 4
NZ = 8
NT = (((1,), (1,)), ((), ()))


def kernel(
    scale,
    inputs_ref, targets_ref, wenc_ref, benc_ref, wdec_ref,
    genc_ref, gdec_ref, gb_ref,
    x_in, w_en, b_en, t_in, w_all, act_t, a_mat, pre_s, part, y_out, y_in,
    zp_out, zm_out, zp_in, zm_in, x_out, x_sum, x_rec, err, grads, zeros, acc, acc_in, ge_out, gb_out,
    load_sem, zero_sem, store_sem, fin_sem,
    w_s, w_r, t_s, t_r, a_s, a_r, c_s, c_r, g_s, g_r,
    y_s, y_r, zp_s, zp_r, zm_s, zm_r, x_s, x_r, e_s, e_r, ep_s, ep_r, em_s, em_r, b_s, b_r,
):
    lay = lax.axis_index("layer")
    ft = lax.axis_index("feat")
    y_lo = lay // NX
    x = lay % NX
    z = ft // 4
    y_hi = (ft // 2) % 2
    c = ft % 2
    half = w_all.shape[2]
    slab = wdec_ref.shape[1]

    def feat_of(zz, hh):
        return zz * 4 + hh * 2 + c

    partner = (lay, ft + 1 - 2 * c)
    z_up = (lay, feat_of((z + 1) % NZ, y_hi))
    z_dn = (lay, feat_of((z + NZ - 1) % NZ, y_hi))
    other_lay = (1 - y_lo) * NX + x
    my_cols = pl.ds(pl.multiple_of(c * half, 128), half)
    their_cols = pl.ds(pl.multiple_of((1 - c) * half, 128), half)

    def remote(src, dst, s, r, dev):
        return pltpu.make_async_remote_copy(
            src_ref=src, dst_ref=dst, send_sem=s, recv_sem=r, device_id=dev, device_id_type=MESH
        )

    ld_w = [
        pltpu.make_async_copy(wenc_ref, w_en, load_sem.at[0]),
        pltpu.make_async_copy(inputs_ref, x_in, load_sem.at[1]),
        pltpu.make_async_copy(benc_ref, b_en, load_sem.at[2]),
        pltpu.make_async_copy(targets_ref, t_in.at[0], load_sem.at[3]),
    ]
    for d in ld_w:
        d.start()

    def own_w(m):
        return pltpu.make_async_copy(
            wdec_ref.at[m, :, my_cols], w_all.at[m, pl.ds(0, slab), :], load_sem.at[4 + m]
        )

    def load_body(m, _):
        own_w(m).start()
        return 0

    lax.fori_loop(lay, 8, load_body, 0)

    barrier = pltpu.get_barrier_semaphore()

    def greet(dev):
        pl.semaphore_signal(barrier, inc=1, device_id=dev, device_id_type=MESH)

    greet(partner)
    greet(z_up)
    greet(z_dn)
    greet((other_lay, feat_of(z, y_hi)))
    greet((other_lay, feat_of(z, 1 - y_hi)))
    for k in range(1, NX):
        mate = y_lo * NX + (x + k) % NX
        greet((mate, feat_of(z, y_hi)))
        greet((mate, feat_of(z, 1 - y_hi)))
    greet((lay, feat_of(z, 1 - y_hi)))
    zeros[...] = jnp.zeros_like(zeros)
    pl.semaphore_wait(barrier, 12)

    def swap_w(m):
        return remote(
            wdec_ref.at[m, :, their_cols], w_all.at[m, pl.ds(slab, slab), :], w_s.at[m], w_r.at[m], partner
        )

    swap_t = remote(targets_ref, t_in.at[1], t_s, t_r, partner)
    swap_t.start()

    def swap_body(k, _):
        swap_w(7 - k).start()
        return 0

    lax.fori_loop(0, 8 - lay, swap_body, 0)

    def zero_copy(m):
        return pltpu.make_async_copy(zeros, gdec_ref.at[m], zero_sem.at[m])

    def zero_body(m, _):
        zero_copy(m).start()
        return 0

    lax.fori_loop(0, lay, zero_body, 0)

    row = lax.broadcasted_iota(jnp.int32, (slab, slab), 0)
    col = lax.broadcasted_iota(jnp.int32, (slab, slab), 1)
    ld_w[2].wait()
    bias = jnp.sum(jnp.where(row == col, b_en[...], 0.0), axis=1, keepdims=True)
    ld_w[0].wait()
    ld_w[1].wait()
    pre = lax.dot_general(w_en[...], x_in[...], NT, preferred_element_type=F32) + bias
    pre_s[...] = pre
    act_t[pl.ds(0, slab), :] = jnp.maximum(pre, 0.0).astype(BF16)
    swap_a = remote(act_t.at[pl.ds(0, slab), :], act_t.at[pl.ds(slab, slab), :], a_s, a_r, partner)
    swap_a.start()
    ld_w[3].wait()
    swap_t.wait_recv()
    swap_a.wait_recv()
    a_mat[...] = act_t[...].T

    chunk = 384

    def wait_w(m):
        own_w(m).wait()
        swap_w(m).wait_recv()

    def y_copy(j, tb):
        dev = (other_lay, feat_of(z, (y_hi + tb) % 2))
        return remote(y_out.at[j, tb], y_in.at[j, tb], y_s.at[j, tb], y_r.at[j, tb], dev)

    order = (4, NZ - 3, 3, NZ - 2, 2, NZ - 1, 1, 0)

    @pl.when(y_lo == 0)
    def _():
        def up_body(j, _):
            m = NX + j
            wait_w(m)
            for n in range(0, half, chunk):
                p = jnp.dot(a_mat[...], w_all[m, :, pl.ds(n, chunk)], preferred_element_type=F32)
                y_out[j, :, :, pl.ds(n, chunk)] = p.astype(BF16).reshape(NZ, 16, chunk)
            return 0

        lax.fori_loop(0, NX, up_body, 0)
        for off in order:
            tb = (z + off) % NZ

            def send_body(j, _):
                y_copy(j, tb).start()
                return 0

            lax.fori_loop(0, NX, send_body, 0)

    lo = jnp.where(y_lo == 1, 0, x)
    n_act = NX - lo

    def row_body(j, _):
        m = y_lo * NX + j

        @pl.when(m >= lay)
        def _():
            wait_w(m)
            for n in range(0, half, chunk):
                p = jnp.dot(a_mat[...], w_all[m, :, pl.ds(n, chunk)], preferred_element_type=F32)
                part[j, :, :, pl.ds(n, chunk)] = p.reshape(NZ, 16, chunk)

        @pl.when(m < lay)
        def _():
            part[j] = jnp.zeros(part.shape[1:], F32)

        return 0

    lax.fori_loop(lo, NX, row_body, 0)

    @pl.when(z // 4 == c)
    def _():
        width = t_in.shape[1]
        for k in range(2):
            core = c if k == 0 else 1 - c
            start = width * (2 * ((2 * z + y_hi) % NZ) + core)
            tt = t_in[k].astype(F32).T.astype(BF16)
            for n in range(0, half, chunk):
                jj = lax.broadcasted_iota(jnp.int32, (width, chunk), 0) + start
                nn = lax.broadcasted_iota(jnp.int32, (width, chunk), 1) + n
                sel = jnp.where(jj == nn, -1.0, 0.0).astype(BF16)
                t_full = jnp.dot(tt, sel, preferred_element_type=F32)
                part[x, :, :, pl.ds(n, chunk)] = part[x, :, :, pl.ds(n, chunk)] + t_full.reshape(
                    NZ, 16, chunk
                )

    def absorb(j, tb):
        @pl.when(y_lo == 1)
        def _():
            y_copy(j, tb).wait_recv()
            part[j, tb] = part[j, tb] + y_in[j, tb].astype(F32)

    def rs_up(s, j):
        return remote(zp_out.at[s, j], zp_in.at[s, j], zp_s.at[s, j], zp_r.at[s, j], z_up)

    def rs_dn(s, j):
        return remote(zm_out.at[s, j], zm_in.at[s, j], zm_s.at[s, j], zm_r.at[s, j], z_dn)

    for s in range(4):
        t_up = (z + 4 - s) % NZ
        t_dn = (z + NZ - 3 + s) % NZ

        def rs_body(j, _):
            absorb(j, t_up)
            v = part[j, t_up]
            if s > 0:
                rs_up(s - 1, j).wait_recv()
                v = v + zp_in[s - 1, j].astype(F32)
            zp_out[s, j] = v.astype(BF16)
            rs_up(s, j).start()
            if s < 3:
                absorb(j, t_dn)
                w = part[j, t_dn]
                if s > 0:
                    rs_dn(s - 1, j).wait_recv()
                    w = w + zm_in[s - 1, j].astype(F32)
                zm_out[s, j] = w.astype(BF16)
                rs_dn(s, j).start()
            return 0

        lax.fori_loop(lo, NX, rs_body, 0)

    def x_same(j):
        return remote(
            x_out.at[j], x_rec.at[x], x_s.at[j], x_r.at[x], (y_lo * NX + j, feat_of(z, y_hi))
        )

    def x_twin(j):
        return remote(
            x_out.at[j], x_rec.at[NX + x], x_s.at[NX + j], x_r.at[NX + x], (y_lo * NX + j, feat_of(z, 1 - y_hi))
        )

    def x_wait(slot):
        remote(x_out.at[0], x_rec.at[slot], x_s.at[0], x_r.at[slot], partner).wait_recv()

    def x_body(j, _):
        absorb(j, z)
        rs_dn(2, j).wait_recv()
        rs_up(3, j).wait_recv()
        v = part[j, z] + zm_in[2, j].astype(F32) + zp_in[3, j].astype(F32)
        x_out[j] = v.astype(BF16)
        x_twin(j).start()

        @pl.when(j != x)
        def _():
            x_same(j).start()

        @pl.when(j == x)
        def _():
            x_sum[...] = v

        return 0

    lax.fori_loop(lo, NX, x_body, 0)

    n_src = jnp.where(y_lo == 1, NX, x + 1)

    def sum_body(xx, _):
        @pl.when(xx != x)
        def _():
            x_wait(xx)
            x_sum[...] = x_sum[...] + x_rec[xx].astype(F32)

        x_wait(NX + xx)
        x_sum[...] = x_sum[...] + x_rec[NX + xx].astype(F32)
        return 0

    lax.fori_loop(0, n_src, sum_body, 0)
    err[lay, z] = x_sum[...].astype(BF16)

    def e_send(xx):
        return remote(
            err.at[lay, z], err.at[lay, z], e_s.at[xx], e_r.at[x], (y_lo * NX + xx, feat_of(z, y_hi))
        )

    def e_wait(j):
        remote(err.at[lay, z], err.at[y_lo * NX + j, z], e_s.at[0], e_r.at[j], partner).wait_recv()

    n_dst = jnp.where(y_lo == 1, NX, x)

    def e_body(xx, _):
        @pl.when(xx != x)
        def _():
            e_send(xx).start()

        return 0

    lax.fori_loop(0, n_dst, e_body, 0)

    def ag_up(s, j, tb):
        piece = err.at[y_lo * NX + j, tb]
        return remote(piece, piece, ep_s.at[s, j], ep_r.at[s, j], z_up)

    def ag_dn(s, j, tb):
        piece = err.at[y_lo * NX + j, tb]
        return remote(piece, piece, em_s.at[s, j], em_r.at[s, j], z_dn)

    def back(j, tb):
        piece = err.at[NX + j, tb]
        return remote(
            piece, piece, b_s.at[j, tb], b_r.at[j, tb], (other_lay, feat_of(z, (y_hi + tb) % 2))
        )

    def forward_back(j, tb):
        @pl.when(y_lo == 1)
        def _():
            back(j, tb).start()

    def gdec_own(m):
        return pltpu.make_async_copy(
            grads.at[m, pl.ds(0, slab), :], gdec_ref.at[m, :, my_cols], store_sem.at[m]
        )

    def gdec_peer(m):
        return remote(
            grads.at[m, pl.ds(slab, slab), :], gdec_ref.at[m, :, my_cols], g_s.at[m], g_r.at[m], partner
        )

    def gdec_wait(m):
        remote(
            grads.at[m, pl.ds(slab, slab), :], gdec_ref.at[m, :, their_cols], g_s.at[m], g_r.at[m], partner
        ).wait_recv()

    acc[...] = jnp.zeros_like(acc)

    def backward(m):
        for n in range(0, half, chunk):
            e = err[m, :, :, pl.ds(n, chunk)].reshape(NZ * 16, chunk)
            g = jnp.dot(act_t[...], e, preferred_element_type=F32) * scale
            grads[m, :, pl.ds(n, chunk)] = g.astype(BF16)
        gdec_peer(m).start()
        gdec_own(m).start()
        e = err[m].reshape(NZ * 16, half)
        acc[...] = acc[...] + lax.dot_general(w_all[m], e, NT, preferred_element_type=F32)

    for s in range(5):
        t_up = (z + NZ - s) % NZ
        t_dn = (z + s) % NZ

        def ag_body(k, _):
            j = (x + k) % NX
            if s == 0:

                @pl.when(k > 0)
                def _():
                    e_wait(j)

                ag_up(0, j, z).start()
                ag_dn(0, j, z).start()
                forward_back(j, z)
            else:
                ag_up(s - 1, j, t_up).wait_recv()
                if s < 4:
                    ag_up(s, j, t_up).start()
                forward_back(j, t_up)
                if s < 4:
                    ag_dn(s - 1, j, t_dn).wait_recv()
                    if s < 3:
                        ag_dn(s, j, t_dn).start()
                    forward_back(j, t_dn)
            if s == 4:

                @pl.when(j >= x)
                def _():
                    backward(y_lo * NX + j)

            return 0

        lax.fori_loop(0, n_act, ag_body, 0)

    @pl.when(y_lo == 0)
    def _():
        def up_back(j, _):
            def wait_body(tb, _):
                back(j, tb).wait_recv()
                return 0

            lax.fori_loop(0, NZ, wait_body, 0)
            backward(NX + j)
            return 0

        lax.fori_loop(0, NX, up_back, 0)

    swap_c = remote(acc.at[pl.ds(slab, slab), :], acc_in, c_s, c_r, partner)
    swap_c.start()
    swap_c.wait_recv()
    act_grad = (acc[pl.ds(0, slab), :] + acc_in[...]) * scale
    pre_grad = jnp.where(pre_s[...] > 0.0, act_grad, 0.0).astype(BF16)
    ge_out[...] = jnp.dot(pre_grad, x_in[...], preferred_element_type=F32).astype(BF16)
    total = jnp.sum(pre_grad.astype(F32), axis=1, keepdims=True)
    gb_out[...] = jnp.sum(jnp.where(row == col, total, 0.0), axis=0, keepdims=True)
    st_e = pltpu.make_async_copy(ge_out, genc_ref, fin_sem.at[0])
    st_b = pltpu.make_async_copy(gb_out, gb_ref, fin_sem.at[1])
    st_e.start()
    st_b.start()

    swap_t.wait_send()
    swap_a.wait_send()
    swap_c.wait_send()

    def own_done(m, _):
        swap_w(m).wait_send()
        gdec_own(m).wait()
        gdec_peer(m).wait_send()
        gdec_wait(m)
        return 0

    lax.fori_loop(lay, 8, own_done, 0)

    def zero_done(m, _):
        zero_copy(m).wait()
        return 0

    lax.fori_loop(0, lay, zero_done, 0)

    def chain_done(j, _):
        for s in range(4):
            rs_up(s, j).wait_send()
            ag_up(s, j, z).wait_send()
        for s in range(3):
            rs_dn(s, j).wait_send()
            ag_dn(s, j, z).wait_send()
        x_twin(j).wait_send()

        @pl.when(j != x)
        def _():
            x_same(j).wait_send()

        return 0

    lax.fori_loop(lo, NX, chain_done, 0)

    def e_done(xx, _):
        @pl.when(xx != x)
        def _():
            e_send(xx).wait_send()

        return 0

    lax.fori_loop(0, n_dst, e_done, 0)

    def y_done(i, _):
        @pl.when(y_lo == 0)
        def _():
            y_copy(i // NZ, i % NZ).wait_send()

        @pl.when(y_lo == 1)
        def _():
            back(i // NZ, i % NZ).wait_send()

        return 0

    lax.fori_loop(0, NX * NZ, y_done, 0)
    st_e.wait()
    st_b.wait()


def shards(inputs, targets, w_enc, b_enc, w_dec):
    tok, width = inputs.shape[1], inputs.shape[2]
    n_lay, slab = w_dec.shape[1], w_dec.shape[2]
    half = width // 2
    tcols = targets.shape[2]
    dma = pltpu.SemaphoreType.DMA
    vm = pltpu.VMEM
    any_spec = pl.BlockSpec(memory_space=pl.ANY)
    piece = (16, half)
    outs = pl.pallas_call(
        functools.partial(kernel, tok ** (-0.5)),
        out_shape=(
            jax.ShapeDtypeStruct((slab, width), BF16),
            jax.ShapeDtypeStruct((n_lay, slab, width), BF16),
            jax.ShapeDtypeStruct((1, slab), F32),
        ),
        in_specs=[any_spec] * 5,
        out_specs=(any_spec,) * 3,
        scratch_shapes=[
            vm((tok, width), BF16),
            vm((slab, width), BF16),
            vm((1, slab), F32),
            vm((2, tcols, tok), BF16),
            vm((n_lay, 2 * slab, half), BF16),
            vm((2 * slab, tok), BF16),
            vm((tok, 2 * slab), BF16),
            vm((slab, tok), F32),
            vm((NX, NZ) + piece, F32),
            vm((NX, NZ) + piece, BF16),
            vm((NX, NZ) + piece, BF16),
            vm((4, NX) + piece, BF16),
            vm((3, NX) + piece, BF16),
            vm((4, NX) + piece, BF16),
            vm((3, NX) + piece, BF16),
            vm((NX,) + piece, BF16),
            vm(piece, F32),
            vm((2 * NX,) + piece, BF16),
            vm((n_lay, NZ) + piece, BF16),
            vm((n_lay, 2 * slab, half), BF16),
            vm((slab, width), BF16),
            vm((2 * slab, tok), F32),
            vm((slab, tok), F32),
            vm((slab, width), BF16),
            vm((1, slab), F32),
            dma((4 + n_lay,)),
            dma((n_lay,)),
            dma((n_lay,)),
            dma((2,)),
            dma((n_lay,)), dma((n_lay,)),
            dma, dma,
            dma, dma,
            dma, dma,
            dma((n_lay,)), dma((n_lay,)),
            dma((NX, NZ)), dma((NX, NZ)),
            dma((4, NX)), dma((4, NX)),
            dma((3, NX)), dma((3, NX)),
            dma((2 * NX,)), dma((2 * NX,)),
            dma((NX,)), dma((NX,)),
            dma((4, NX)), dma((4, NX)),
            dma((3, NX)), dma((3, NX)),
            dma((NX, NZ)), dma((NX, NZ)),
        ],
        compiler_params=pltpu.CompilerParams(
            collective_id=0, has_side_effects=True, vmem_limit_bytes=48 * 1024 * 1024
        ),
    )(inputs[0], targets[0].T, w_enc[0].T, b_enc, w_dec[0])
    genc, gdec, gb = outs
    return genc.T[None], gdec[None], gb


def solution(mesh):
    in_specs = (
        P("layer", None, None),
        P("layer", None, "feat"),
        P("layer", None, "feat"),
        P("layer", "feat"),
        P("layer", None, "feat", None),
    )
    out_specs = (P("layer", None, "feat"), P("layer", None, "feat", None), P("layer", "feat"))
    return jax.shard_map(shards, mesh=mesh, in_specs=in_specs, out_specs=out_specs, check_vma=False)
```

time: 1770 us -> 74.7 us (0.04)
  waiting for transfers between devices: 1710 us -> 0 us
  Pallas kernels: 0 us -> 64.9 us
  matrix products: 21.3 us -> 0 us
    unnamed x3 -> x0, waiting for transfers between devices: 1290 us -> none
    all_gather x1 -> x0, waiting for transfers between devices: 415 us -> none  [shards(): lax.all_gather(err_block, ('layer', 'feat'), axis=0, tiled=True)]
    pallas_call x0 -> x1, Pallas kernels: none -> 64.9 us  [shards(): pl.pallas_call(functools.partial(kernel, tok ** (-0.5)), out_shape=(jax.S...]
    dot_general x5 -> x0, matrix products: 21.3 us -> none  [the longest x1 8.69 us: shards(): jnp.einsum('tf,mfnc->mntc', active, blocks, preferred_element_type=jnp.fl...]
    another operation x2 -> x0, local copies, waits for them, and re-layouts: 19.5 us -> none  [the longest x1 11.4 us: shards(): blocks = weights.reshape(layer_count, slab_width, feat_count, col_count)]
  transfers between devices with their start and end apart: 2 -> 0, of which waited for: 2 -> 0; matrix products, arithmetic and copies ran while one was open for 0% -> 0% of each run, Pallas kernels for 0% -> 0%
where the time goes in v1:
time: 74.7 us; the launch traced here: 73.2 us
  Pallas kernels  64.9 us (87%)
  local copies, waits for them, and re-layouts  7.69 us (10%)
    pallas_call x1, Pallas kernels, shards(): pl.pallas_call(functools.partial(kernel, tok ** (-0.5)), out_shape=(jax.S...  64.9 us
    unnamed x13, local copies, waits for them, and re-layouts  7.69 us

profile of v1, /device:TPU:1, one launch (start us, length us, event | category | flops | bytes accessed | tf_op | source)
XLA Modules:
  0.0 73.2 jit_solution(4530393789254622495)
XLA Ops:
  0.6 0.0 copy-start
  0.6 1.7 %copy-done = bf16[1,8,64,2304]{3,2,1,0:T(8,128)(2,1)S(1)} copy-done((bf16[1,8,64,2304]{3,2,1,0:T(8,128)(2,1)S(1)}, bf16[1,8,64,2304]{3,2,1,0:T(8,128)(2,1)}, u32[]{:S(2)}) %copy-start) | copy-done | bytes 2359320
  2.3 0.0 copy-start.1
  2.3 1.1 %copy-done.1 = bf16[1,128,2304]{2,1,0:T(8,128)(2,1)S(1)} copy-done((bf16[1,128,2304]{2,1,0:T(8,128)(2,1)S(1)}, bf16[1,128,2304]{2,1,0:T(8,128)(2,1)}, u32[]{:S(2)}) %copy-start.1) | copy-done | bytes 589848
  3.4 0.0 copy-start.2
  3.4 1.0 %copy-done.2 = bf16[1,2304,64]{1,2,0:T(8,128)(2,1)S(1)} copy-done((bf16[1,2304,64]{1,2,0:T(8,128)(2,1)S(1)}, bf16[1,2304,64]{1,2,0:T(8,128)(2,1)}, u32[]{:S(2)}) %copy-start.2) | copy-done | bytes 294936
  4.3 0.0 copy-start.3
  4.3 0.7 copy-done.3
  5.0 0.0 copy-start.4
  5.0 0.7 copy-done.4
  5.7 64.9 %shard_map.76 = (bf16[64,2304]{1,0:T(8,128)(2,1)S(1)}, bf16[8,64,2304]{2,1,0:T(8,128)(2,1)S(1)}, f32[1,64]{1,0:T(1,128)S(1)}) custom-call(bf16[128,2304]{1,0:T(8,128)(2,1)S(1)} %bitcast.14, bf16[72,128]{1,0:T(8,128)(2,1)S(1)} %bitcast.17, bf16[64,2304]{1,0:T(8,128)(2,1)S(1)} %bitcast.15, f32[1,64]{1,0:T(1,128)S(1)} %copy-done.4, ...), custom_call_target="tpu_custom_call" | custom-call | tf_op jit(solution)/shard_map/pallas_call | solution.py:480
  70.6 0.7 copy.11
  71.3 1.4 %copy.12 = bf16[1,8,64,2304]{3,2,1,0:T(8,128)(2,1)} copy(bf16[1,8,64,2304]{3,2,1,0:T(8,128)(2,1)S(1)} %bitcast.13) | data formatting | bytes 4718592
  72.7 0.5 copy.13
Async XLA Ops:
  0.6 1.7 %copy-start = (bf16[1,8,64,2304]{3,2,1,0:T(8,128)(2,1)S(1)}, bf16[1,8,64,2304]{3,2,1,0:T(8,128)(2,1)}, u32[]{:S(2)}) copy-start(bf16[1,8,64,2304]{3,2,1,0:T(8,128)(2,1)} %param.9) | copy-start | bytes 7077892
  2.3 1.1 %copy-start.1 = (bf16[1,128,2304]{2,1,0:T(8,128)(2,1)S(1)}, bf16[1,128,2304]{2,1,0:T(8,128)(2,1)}, u32[]{:S(2)}) copy-start(bf16[1,128,2304]{2,1,0:T(8,128)(2,1)} %param.5) | copy-start | bytes 1769476
  3.4 1.0 %copy-start.2 = (bf16[1,2304,64]{1,2,0:T(8,128)(2,1)S(1)}, bf16[1,2304,64]{1,2,0:T(8,128)(2,1)}, u32[]{:S(2)}) copy-start(bf16[1,2304,64]{1,2,0:T(8,128)(2,1)} %param.7) | copy-start | bytes 884740
  4.3 0.7 copy-start.3
  5.0 0.7 copy-start.4

commit v2 on v1

--- a/solution.py
+++ b/solution.py
@@ -23,8 +23,8 @@
     x_in, w_en, b_en, t_in, w_all, act_t, a_mat, pre_s, part, y_out, y_in,
     zp_out, zm_out, zp_in, zm_in, x_out, x_sum, x_rec, err, grads, zeros, acc, acc_in, ge_out, gb_out,
     load_sem, zero_sem, store_sem, fin_sem,
-    w_s, w_r, t_s, t_r, a_s, a_r, c_s, c_r, g_s, g_r,
-    y_s, y_r, zp_s, zp_r, zm_s, zm_r, x_s, x_r, e_s, e_r, ep_s, ep_r, em_s, em_r, b_s, b_r,
+    w_s, w_r, t_s, t_r, bb_s, bb_r, a_s, a_r, c_s, c_r, g_s, g_r,
+    y_s, y_r, zp_s, zp_r, zm_s, zm_r, x_s, x_r, e_s, e_r, ed_s, ep_s, ep_r, em_s, em_r, b_s, b_r,
 ):
     lay = lax.axis_index("layer")
     ft = lax.axis_index("feat")
@@ -40,8 +40,15 @@
         return zz * 4 + hh * 2 + c
 
     partner = (lay, ft + 1 - 2 * c)
-    z_up = (lay, feat_of((z + 1) % NZ, y_hi))
-    z_dn = (lay, feat_of((z + NZ - 1) % NZ, y_hi))
+    def way(j):
+        return 1 - 2 * (j % 2)
+
+    def z_up(j):
+        return (z + NZ + way(j)) % NZ
+
+    def z_dn(j):
+        return (z + NZ - way(j)) % NZ
+
     other_lay = (1 - y_lo) * NX + x
     my_cols = pl.ds(pl.multiple_of(c * half, 128), half)
     their_cols = pl.ds(pl.multiple_of((1 - c) * half, 128), half)
@@ -52,9 +59,9 @@
         )
 
     ld_w = [
-        pltpu.make_async_copy(wenc_ref, w_en, load_sem.at[0]),
+        pltpu.make_async_copy(wenc_ref, w_en.at[pl.ds(0, slab), :], load_sem.at[0]),
         pltpu.make_async_copy(inputs_ref, x_in, load_sem.at[1]),
-        pltpu.make_async_copy(benc_ref, b_en, load_sem.at[2]),
+        pltpu.make_async_copy(benc_ref, b_en.at[0], load_sem.at[2]),
         pltpu.make_async_copy(targets_ref, t_in.at[0], load_sem.at[3]),
     ]
     for d in ld_w:
@@ -65,11 +72,15 @@
             wdec_ref.at[m, :, my_cols], w_all.at[m, pl.ds(0, slab), :], load_sem.at[4 + m]
         )
 
-    def load_body(m, _):
-        own_w(m).start()
-        return 0
-
-    lax.fori_loop(lay, 8, load_body, 0)
+    def in_order(start):
+        def body(m, _):
+            start(m)
+            return 0
+
+        lax.fori_loop(jnp.maximum(lay, NX), 2 * NX, body, 0)
+        lax.fori_loop(lay, NX, body, 0)
+
+    in_order(lambda m: own_w(m).start())
 
     barrier = pltpu.get_barrier_semaphore()
 
@@ -77,31 +88,33 @@
         pl.semaphore_signal(barrier, inc=1, device_id=dev, device_id_type=MESH)
 
     greet(partner)
-    greet(z_up)
-    greet(z_dn)
+    greet((lay, feat_of(z_up(0), y_hi)))
+    greet((lay, feat_of(z_dn(0), y_hi)))
     greet((other_lay, feat_of(z, y_hi)))
     greet((other_lay, feat_of(z, 1 - y_hi)))
     for k in range(1, NX):
         mate = y_lo * NX + (x + k) % NX
         greet((mate, feat_of(z, y_hi)))
         greet((mate, feat_of(z, 1 - y_hi)))
+        greet((mate, feat_of((z + 1) % NZ, y_hi)))
+        greet((mate, feat_of((z + NZ - 1) % NZ, y_hi)))
     greet((lay, feat_of(z, 1 - y_hi)))
     zeros[...] = jnp.zeros_like(zeros)
-    pl.semaphore_wait(barrier, 12)
+    pl.semaphore_wait(barrier, 18)
 
     def swap_w(m):
         return remote(
             wdec_ref.at[m, :, their_cols], w_all.at[m, pl.ds(slab, slab), :], w_s.at[m], w_r.at[m], partner
         )
 
+    swap_e = remote(wenc_ref, w_en.at[pl.ds(slab, slab), :], a_s, a_r, partner)
+    swap_e.start()
+    swap_b = remote(benc_ref, b_en.at[1], bb_s, bb_r, partner)
+    swap_b.start()
     swap_t = remote(targets_ref, t_in.at[1], t_s, t_r, partner)
     swap_t.start()
 
-    def swap_body(k, _):
-        swap_w(7 - k).start()
-        return 0
-
-    lax.fori_loop(0, 8 - lay, swap_body, 0)
+    in_order(lambda m: swap_w(m).start())
 
     def zero_copy(m):
         return pltpu.make_async_copy(zeros, gdec_ref.at[m], zero_sem.at[m])
@@ -115,18 +128,20 @@
     row = lax.broadcasted_iota(jnp.int32, (slab, slab), 0)
     col = lax.broadcasted_iota(jnp.int32, (slab, slab), 1)
     ld_w[2].wait()
-    bias = jnp.sum(jnp.where(row == col, b_en[...], 0.0), axis=1, keepdims=True)
+    swap_b.wait_recv()
+    bias = jnp.concatenate(
+        [jnp.sum(jnp.where(row == col, b_en[i], 0.0), axis=1, keepdims=True) for i in range(2)], axis=0
+    )
     ld_w[0].wait()
     ld_w[1].wait()
+    swap_e.wait_recv()
     pre = lax.dot_general(w_en[...], x_in[...], NT, preferred_element_type=F32) + bias
-    pre_s[...] = pre
-    act_t[pl.ds(0, slab), :] = jnp.maximum(pre, 0.0).astype(BF16)
-    swap_a = remote(act_t.at[pl.ds(0, slab), :], act_t.at[pl.ds(slab, slab), :], a_s, a_r, partner)
-    swap_a.start()
+    pre_s[...] = pre[:slab]
+    act = jnp.maximum(pre, 0.0).astype(BF16)
+    act_t[...] = act
+    a_mat[...] = act.T
     ld_w[3].wait()
     swap_t.wait_recv()
-    swap_a.wait_recv()
-    a_mat[...] = act_t[...].T
 
     chunk = 384
 
@@ -138,7 +153,7 @@
         dev = (other_lay, feat_of(z, (y_hi + tb) % 2))
         return remote(y_out.at[j, tb], y_in.at[j, tb], y_s.at[j, tb], y_r.at[j, tb], dev)
 
-    order = (4, NZ - 3, 3, NZ - 2, 2, NZ - 1, 1, 0)
+    order = (4, -3, 3, -2, 2, -1, 1, 0)
 
     @pl.when(y_lo == 0)
     def _():
@@ -148,22 +163,22 @@
             for n in range(0, half, chunk):
                 p = jnp.dot(a_mat[...], w_all[m, :, pl.ds(n, chunk)], preferred_element_type=F32)
                 y_out[j, :, :, pl.ds(n, chunk)] = p.astype(BF16).reshape(NZ, 16, chunk)
+            for off in order[:2]:
+                y_copy(j, (z + NZ + way(j) * off) % NZ).start()
             return 0
 
         lax.fori_loop(0, NX, up_body, 0)
-        for off in order:
-            tb = (z + off) % NZ
+        for off in order[2:]:
 
             def send_body(j, _):
-                y_copy(j, tb).start()
+                y_copy(j, (z + NZ + way(j) * off) % NZ).start()
                 return 0
 
             lax.fori_loop(0, NX, send_body, 0)
 
     lo = jnp.where(y_lo == 1, 0, x)
-    n_act = NX - lo
-
-    def row_body(j, _):
+
+    def row_part(j):
         m = y_lo * NX + j
 
         @pl.when(m >= lay)
@@ -177,25 +192,21 @@
         def _():
             part[j] = jnp.zeros(part.shape[1:], F32)
 
-        return 0
-
-    lax.fori_loop(lo, NX, row_body, 0)
-
-    @pl.when(z // 4 == c)
-    def _():
-        width = t_in.shape[1]
-        for k in range(2):
-            core = c if k == 0 else 1 - c
-            start = width * (2 * ((2 * z + y_hi) % NZ) + core)
-            tt = t_in[k].astype(F32).T.astype(BF16)
-            for n in range(0, half, chunk):
-                jj = lax.broadcasted_iota(jnp.int32, (width, chunk), 0) + start
-                nn = lax.broadcasted_iota(jnp.int32, (width, chunk), 1) + n
-                sel = jnp.where(jj == nn, -1.0, 0.0).astype(BF16)
-                t_full = jnp.dot(tt, sel, preferred_element_type=F32)
-                part[x, :, :, pl.ds(n, chunk)] = part[x, :, :, pl.ds(n, chunk)] + t_full.reshape(
-                    NZ, 16, chunk
-                )
+        @pl.when((z // 4 == c) & (j == x))
+        def _():
+            width = t_in.shape[1]
+            for k in range(2):
+                core = c if k == 0 else 1 - c
+                start = width * (2 * ((2 * z + y_hi) % NZ) + core)
+                tt = t_in[k].astype(F32).T.astype(BF16)
+                for n in range(0, half, chunk):
+                    jj = lax.broadcasted_iota(jnp.int32, (width, chunk), 0) + start
+                    nn = lax.broadcasted_iota(jnp.int32, (width, chunk), 1) + n
+                    sel = jnp.where(jj == nn, -1.0, 0.0).astype(BF16)
+                    t_full = jnp.dot(tt, sel, preferred_element_type=F32)
+                    part[x, :, :, pl.ds(n, chunk)] = part[x, :, :, pl.ds(n, chunk)] + t_full.reshape(
+                        NZ, 16, chunk
+                    )
 
     def absorb(j, tb):
         @pl.when(y_lo == 1)
@@ -204,16 +215,18 @@
             part[j, tb] = part[j, tb] + y_in[j, tb].astype(F32)
 
     def rs_up(s, j):
-        return remote(zp_out.at[s, j], zp_in.at[s, j], zp_s.at[s, j], zp_r.at[s, j], z_up)
+        return remote(zp_out.at[s, j], zp_in.at[s, j], zp_s.at[s, j], zp_r.at[s, j], (lay, feat_of(z_up(j), y_hi)))
 
     def rs_dn(s, j):
-        return remote(zm_out.at[s, j], zm_in.at[s, j], zm_s.at[s, j], zm_r.at[s, j], z_dn)
+        return remote(zm_out.at[s, j], zm_in.at[s, j], zm_s.at[s, j], zm_r.at[s, j], (lay, feat_of(z_dn(j), y_hi)))
 
     for s in range(4):
-        t_up = (z + 4 - s) % NZ
-        t_dn = (z + NZ - 3 + s) % NZ
 
         def rs_body(j, _):
+            t_up = (z + NZ + way(j) * (4 - s)) % NZ
+            t_dn = (z + NZ - way(j) * (3 - s)) % NZ
+            if s == 0:
+                row_part(j)
             absorb(j, t_up)
             v = part[j, t_up]
             if s > 0:
@@ -291,33 +304,52 @@
 
     n_dst = jnp.where(y_lo == 1, NX, x)
 
+    def ag_up(s, j, tb):
+        piece = err.at[y_lo * NX + j, tb]
+        return remote(piece, piece, ep_s.at[s, j], ep_r.at[s, j], (lay, feat_of(z_up(j), y_hi)))
+
+    def ag_dn(s, j, tb):
+        piece = err.at[y_lo * NX + j, tb]
+        return remote(piece, piece, em_s.at[s, j], em_r.at[s, j], (lay, feat_of(z_dn(j), y_hi)))
+
+    def back(j, tb):
+        piece = err.at[NX + j, tb]
+        return remote(
+            piece, piece, b_s.at[j, tb], b_r.at[j, tb], (other_lay, feat_of(z, (y_hi + tb + j) % 2))
+        )
+
+    def forward_back(j, tb):
+        @pl.when(y_lo == 1)
+        def _():
+            back(j, tb).start()
+
+    def e_up(xx):
+        return remote(
+            err.at[lay, z], err.at[lay, z], ed_s.at[0, xx], ep_r.at[0, x], (y_lo * NX + xx, feat_of(z_up(x), y_hi))
+        )
+
+    def e_dn(xx):
+        return remote(
+            err.at[lay, z], err.at[lay, z], ed_s.at[1, xx], em_r.at[0, x], (y_lo * NX + xx, feat_of(z_dn(x), y_hi))
+        )
+
+    ag_up(0, x, z).start()
+    ag_dn(0, x, z).start()
+
     def e_body(xx, _):
         @pl.when(xx != x)
         def _():
+            @pl.when((xx + x) % 2 == 1)
+            def _():
+                e_up(xx).start()
+                e_dn(xx).start()
+
             e_send(xx).start()
 
         return 0
 
     lax.fori_loop(0, n_dst, e_body, 0)
-
-    def ag_up(s, j, tb):
-        piece = err.at[y_lo * NX + j, tb]
-        return remote(piece, piece, ep_s.at[s, j], ep_r.at[s, j], z_up)
-
-    def ag_dn(s, j, tb):
-        piece = err.at[y_lo * NX + j, tb]
-        return remote(piece, piece, em_s.at[s, j], em_r.at[s, j], z_dn)
-
-    def back(j, tb):
-        piece = err.at[NX + j, tb]
-        return remote(
-            piece, piece, b_s.at[j, tb], b_r.at[j, tb], (other_lay, feat_of(z, (y_hi + tb) % 2))
-        )
-
-    def forward_back(j, tb):
-        @pl.when(y_lo == 1)
-        def _():
-            back(j, tb).start()
+    forward_back(x, z)
 
     def gdec_own(m):
         return pltpu.make_async_copy(
@@ -336,31 +368,40 @@
 
     acc[...] = jnp.zeros_like(acc)
 
-    def backward(m):
+    def decoder_grad(m):
         for n in range(0, half, chunk):
             e = err[m, :, :, pl.ds(n, chunk)].reshape(NZ * 16, chunk)
             g = jnp.dot(act_t[...], e, preferred_element_type=F32) * scale
             grads[m, :, pl.ds(n, chunk)] = g.astype(BF16)
         gdec_peer(m).start()
         gdec_own(m).start()
+
+    def backward(m):
         e = err[m].reshape(NZ * 16, half)
         acc[...] = acc[...] + lax.dot_general(w_all[m], e, NT, preferred_element_type=F32)
 
+        @pl.when(m < 2 * NX - 1)
+        def _():
+            decoder_grad(m)
+
     for s in range(5):
-        t_up = (z + NZ - s) % NZ
-        t_dn = (z + s) % NZ
-
-        def ag_body(k, _):
-            j = (x + k) % NX
+
+        def ag_body(j, _):
+            t_up = (z + NZ - way(j) * s) % NZ
+            t_dn = (z + NZ + way(j) * s) % NZ
             if s == 0:
 
-                @pl.when(k > 0)
+                @pl.when(j != x)
                 def _():
                     e_wait(j)
 
-                ag_up(0, j, z).start()
-                ag_dn(0, j, z).start()
-                forward_back(j, z)
+                    @pl.when((j + x) % 2 == 0)
+                    def _():
+                        ag_up(0, j, z).start()
+                        ag_dn(0, j, z).start()
+
+                    forward_back(j, z)
+
             else:
                 ag_up(s - 1, j, t_up).wait_recv()
                 if s < 4:
@@ -371,15 +412,15 @@
                     if s < 3:
                         ag_dn(s, j, t_dn).start()
                     forward_back(j, t_dn)
-            if s == 4:
-
-                @pl.when(j >= x)
-                def _():
-                    backward(y_lo * NX + j)
-
             return 0
 
-        lax.fori_loop(0, n_act, ag_body, 0)
+        lax.fori_loop(lo, NX, ag_body, 0)
+
+    def row_back(j, _):
+        backward(y_lo * NX + j)
+        return 0
+
+    lax.fori_loop(x, NX, row_back, 0)
 
     @pl.when(y_lo == 0)
     def _():
@@ -396,6 +437,7 @@
 
     swap_c = remote(acc.at[pl.ds(slab, slab), :], acc_in, c_s, c_r, partner)
     swap_c.start()
+    decoder_grad(2 * NX - 1)
     swap_c.wait_recv()
     act_grad = (acc[pl.ds(0, slab), :] + acc_in[...]) * scale
     pre_grad = jnp.where(pre_s[...] > 0.0, act_grad, 0.0).astype(BF16)
@@ -408,7 +450,8 @@
     st_b.start()
 
     swap_t.wait_send()
-    swap_a.wait_send()
+    swap_e.wait_send()
+    swap_b.wait_send()
     swap_c.wait_send()
 
     def own_done(m, _):
@@ -427,12 +470,19 @@
     lax.fori_loop(0, lay, zero_done, 0)
 
     def chain_done(j, _):
+        @pl.when((j + x) % 2 == 0)
+        def _():
+            ag_up(0, j, z).wait_send()
+            ag_dn(0, j, z).wait_send()
+
         for s in range(4):
             rs_up(s, j).wait_send()
-            ag_up(s, j, z).wait_send()
+            if s > 0:
+                ag_up(s, j, z).wait_send()
         for s in range(3):
             rs_dn(s, j).wait_send()
-            ag_dn(s, j, z).wait_send()
+            if s > 0:
+                ag_dn(s, j, z).wait_send()
         x_twin(j).wait_send()
 
         @pl.when(j != x)
@@ -447,6 +497,11 @@
         @pl.when(xx != x)
         def _():
             e_send(xx).wait_send()
+
+            @pl.when((xx + x) % 2 == 1)
+            def _():
+                e_up(xx).wait_send()
+                e_dn(xx).wait_send()
 
         return 0
 
@@ -466,6 +521,15 @@
     lax.fori_loop(0, NX * NZ, y_done, 0)
     st_e.wait()
     st_b.wait()
+
+
+def copy_out(a_ref, b_ref, c_ref, a_out, b_out, c_out, sem):
+    pairs = ((b_ref, b_out), (a_ref, a_out), (c_ref, c_out))
+    copies = [pltpu.make_async_copy(src, dst, sem.at[i]) for i, (src, dst) in enumerate(pairs)]
+    for d in copies:
+        d.start()
+    for d in copies:
+        d.wait()
 
 
 def shards(inputs, targets, w_enc, b_enc, w_dec):
@@ -484,12 +548,12 @@
             jax.ShapeDtypeStruct((n_lay, slab, width), BF16),
             jax.ShapeDtypeStruct((1, slab), F32),
         ),
-        in_specs=[any_spec] * 5,
+        in_specs=[pl.BlockSpec(memory_space=pltpu.HBM)] * 5,
         out_specs=(any_spec,) * 3,
         scratch_shapes=[
             vm((tok, width), BF16),
-            vm((slab, width), BF16),
-            vm((1, slab), F32),
+            vm((2 * slab, width), BF16),
+            vm((2, 1, slab), F32),
             vm((2, tcols, tok), BF16),
             vm((n_lay, 2 * slab, half), BF16),
             vm((2 * slab, tok), BF16),
@@ -520,12 +584,13 @@
             dma, dma,
             dma, dma,
             dma, dma,
+            dma, dma,
             dma((n_lay,)), dma((n_lay,)),
             dma((NX, NZ)), dma((NX, NZ)),
             dma((4, NX)), dma((4, NX)),
             dma((3, NX)), dma((3, NX)),
             dma((2 * NX,)), dma((2 * NX,)),
-            dma((NX,)), dma((NX,)),
+            dma((NX,)), dma((NX,)), dma((2, NX)),
             dma((4, NX)), dma((4, NX)),
             dma((3, NX)), dma((3, NX)),
             dma((NX, NZ)), dma((NX, NZ)),
@@ -533,8 +598,15 @@
         compiler_params=pltpu.CompilerParams(
             collective_id=0, has_side_effects=True, vmem_limit_bytes=48 * 1024 * 1024
         ),
-    )(inputs[0], targets[0].T, w_enc[0].T, b_enc, w_dec[0])
-    genc, gdec, gb = outs
+    )(*(pltpu.with_memory_space_constraint(a, pltpu.HBM) for a in (inputs[0], targets[0].T, w_enc[0].T, b_enc, w_dec[0])))
+    genc, gdec, gb = pl.pallas_call(
+        copy_out,
+        out_shape=tuple(jax.ShapeDtypeStruct(o.shape, o.dtype) for o in outs),
+        in_specs=[any_spec] * 3,
+        out_specs=(pl.BlockSpec(memory_space=pltpu.HBM),) * 3,
+        scratch_shapes=[dma((3,))],
+        compiler_params=pltpu.CompilerParams(vmem_limit_bytes=1024 * 1024),
+    )(*outs)
     return genc.T[None], gdec[None], gb
 
 

time: 74.7 us -> 65.1 us (0.87); the launches traced: 73.2 us -> 65 us
  local copies, waits for them, and re-layouts: 7.69 us -> 0 us
    unnamed x13 -> x0, local copies, waits for them, and re-layouts: 7.69 us -> none
    pallas_call x1, Pallas kernels: 64.9 us -> 62.8 us  [shards(): pl.pallas_call(functools.partial(kernel, tok ** (-0.5)), out_shape=(jax.S...]
    pallas_call x0 -> x1, Pallas kernels: none -> 1.52 us  [shards(): pl.pallas_call(copy_out, out_shape=tuple((jax.ShapeDtypeStruct(o.shape, o...]
where the time goes in v2:
time: 65.1 us; the launch traced here: 65 us
  Pallas kernels  64.4 us (99%)
    pallas_call x1, Pallas kernels, shards(): pl.pallas_call(functools.partial(kernel, tok ** (-0.5)), out_shape=(jax.S...  62.8 us
    pallas_call x1, Pallas kernels, shards(): pl.pallas_call(copy_out, out_shape=tuple((jax.ShapeDtypeStruct(o.shape, o...  1.52 us

profile of v2, /device:TPU:1, one launch (start us, length us, event | category | flops | bytes accessed | tf_op | source)
XLA Modules:
  0.0 65.0 jit_solution(13802807615117629781)
XLA Ops:
  0.6 62.8 %shard_map.76 = (bf16[64,2304]{1,0:T(8,128)(2,1)S(1)}, bf16[8,64,2304]{2,1,0:T(8,128)(2,1)S(1)}, f32[1,64]{1,0:T(1,128)S(1)}) custom-call(bf16[128,2304]{1,0:T(8,128)(2,1)} %bitcast.13, bf16[72,128]{1,0:T(8,128)(2,1)} %bitcast.15, bf16[64,2304]{1,0:T(8,128)(2,1)} %bitcast.14, f32[1,64]{1,0:T(1,128)} %benc_ref.1, bf16[8,64,2304]{2,1,0:T(8,128)(2,1)} %bitcast.12), custom_call_target="tpu_custom_call" | custom-call | tf_op jit(solution)/shard_map/pallas_call | solution.py:544
  63.5 1.5 %shard_map.77 = (bf16[64,2304]{1,0:T(8,128)(2,1)}, bf16[8,64,2304]{2,1,0:T(8,128)(2,1)}, f32[1,64]{1,0:T(1,128)}) custom-call(bf16[64,2304]{1,0:T(8,128)(2,1)S(1)} %get-tuple-element.9.a_ref, bf16[8,64,2304]{2,1,0:T(8,128)(2,1)S(1)} %get-tuple-element.10.b_ref, f32[1,64]{1,0:T(1,128)S(1)} %get-tuple-element.11.c_ref), custom_call_target="tpu_custom_call" | custom-call | tf_op jit(solution)/shard_map/pallas_call | solution.py:602

commit v3 on v2

--- a/solution.py
+++ b/solution.py
@@ -168,6 +168,8 @@
             return 0
 
         lax.fori_loop(0, NX, up_body, 0)
+
+    def send_rest():
         for off in order[2:]:
 
             def send_body(j, _):
@@ -245,6 +247,8 @@
             return 0
 
         lax.fori_loop(lo, NX, rs_body, 0)
+        if s == 0:
+            pl.when(y_lo == 0)(send_rest)
 
     def x_same(j):
         return remote(
@@ -339,12 +343,13 @@
     def e_body(xx, _):
         @pl.when(xx != x)
         def _():
+            e_send(xx).start()
+
             @pl.when((xx + x) % 2 == 1)
             def _():
                 e_up(xx).start()
                 e_dn(xx).start()
 
-            e_send(xx).start()
 
         return 0
 

time: 65.1 us -> 65.1 us (level)
  no operation moved by 1% of the time
where the time goes in v3:
time: 65.1 us; the launch traced here: 65 us
  Pallas kernels  64.3 us (99%)
    pallas_call x1, Pallas kernels, shards(): pl.pallas_call(functools.partial(kernel, tok ** (-0.5)), out_shape=(jax.S...  62.8 us
    pallas_call x1, Pallas kernels, shards(): pl.pallas_call(copy_out, out_shape=tuple((jax.ShapeDtypeStruct(o.shape, o...  1.52 us

profile of v3, /device:TPU:1, one launch (start us, length us, event | category | flops | bytes accessed | tf_op | source)
XLA Modules:
  0.0 65.0 jit_solution(11220877629264771918)
XLA Ops:
  0.6 62.8 %shard_map.76 = (bf16[64,2304]{1,0:T(8,128)(2,1)S(1)}, bf16[8,64,2304]{2,1,0:T(8,128)(2,1)S(1)}, f32[1,64]{1,0:T(1,128)S(1)}) custom-call(bf16[128,2304]{1,0:T(8,128)(2,1)} %bitcast.13, bf16[72,128]{1,0:T(8,128)(2,1)} %bitcast.15, bf16[64,2304]{1,0:T(8,128)(2,1)} %bitcast.14, f32[1,64]{1,0:T(1,128)} %benc_ref.1, bf16[8,64,2304]{2,1,0:T(8,128)(2,1)} %bitcast.12), custom_call_target="tpu_custom_call" | custom-call | tf_op jit(solution)/shard_map/pallas_call | solution.py:549
  63.5 1.5 %shard_map.77 = (bf16[64,2304]{1,0:T(8,128)(2,1)}, bf16[8,64,2304]{2,1,0:T(8,128)(2,1)}, f32[1,64]{1,0:T(1,128)}) custom-call(bf16[64,2304]{1,0:T(8,128)(2,1)S(1)} %get-tuple-element.9.a_ref, bf16[8,64,2304]{2,1,0:T(8,128)(2,1)S(1)} %get-tuple-element.10.b_ref, f32[1,64]{1,0:T(1,128)S(1)} %get-tuple-element.11.c_ref), custom_call_target="tpu_custom_call" | custom-call | tf_op jit(solution)/shard_map/pallas_call | solution.py:607

commit v4 on v3

--- a/solution.py
+++ b/solution.py
@@ -96,11 +96,12 @@
         mate = y_lo * NX + (x + k) % NX
         greet((mate, feat_of(z, y_hi)))
         greet((mate, feat_of(z, 1 - y_hi)))
-        greet((mate, feat_of((z + 1) % NZ, y_hi)))
-        greet((mate, feat_of((z + NZ - 1) % NZ, y_hi)))
+        if k % 2 == 1:
+            greet((mate, feat_of((z + 1) % NZ, y_hi)))
+            greet((mate, feat_of((z + NZ - 1) % NZ, y_hi)))
     greet((lay, feat_of(z, 1 - y_hi)))
     zeros[...] = jnp.zeros_like(zeros)
-    pl.semaphore_wait(barrier, 18)
+    pl.semaphore_wait(barrier, 16)
 
     def swap_w(m):
         return remote(
@@ -143,7 +144,7 @@
     ld_w[3].wait()
     swap_t.wait_recv()
 
-    chunk = 384
+    chunk = half
 
     def wait_w(m):
         own_w(m).wait()

time: 65.1 us -> 65.1 us (level)
  no operation moved by 1% of the time
where the time goes in v4:
time: 65.1 us; the launch traced here: 65 us
  Pallas kernels  64.4 us (99%)
    pallas_call x1, Pallas kernels, shards(): pl.pallas_call(functools.partial(kernel, tok ** (-0.5)), out_shape=(jax.S...  62.8 us
    pallas_call x1, Pallas kernels, shards(): pl.pallas_call(copy_out, out_shape=tuple((jax.ShapeDtypeStruct(o.shape, o...  1.52 us

profile of v4, /device:TPU:1, one launch (start us, length us, event | category | flops | bytes accessed | tf_op | source)
XLA Modules:
  0.0 65.0 jit_solution(4758657587004466733)
XLA Ops:
  0.6 62.8 %shard_map.76 = (bf16[64,2304]{1,0:T(8,128)(2,1)S(1)}, bf16[8,64,2304]{2,1,0:T(8,128)(2,1)S(1)}, f32[1,64]{1,0:T(1,128)S(1)}) custom-call(bf16[128,2304]{1,0:T(8,128)(2,1)} %bitcast.13, bf16[72,128]{1,0:T(8,128)(2,1)} %bitcast.15, bf16[64,2304]{1,0:T(8,128)(2,1)} %bitcast.14, f32[1,64]{1,0:T(1,128)} %benc_ref.1, bf16[8,64,2304]{2,1,0:T(8,128)(2,1)} %bitcast.12), custom_call_target="tpu_custom_call" | custom-call | tf_op jit(solution)/shard_map/pallas_call | solution.py:550
  63.5 1.5 %shard_map.77 = (bf16[64,2304]{1,0:T(8,128)(2,1)}, bf16[8,64,2304]{2,1,0:T(8,128)(2,1)}, f32[1,64]{1,0:T(1,128)}) custom-call(bf16[64,2304]{1,0:T(8,128)(2,1)S(1)} %get-tuple-element.9.a_ref, bf16[8,64,2304]{2,1,0:T(8,128)(2,1)S(1)} %get-tuple-element.10.b_ref, f32[1,64]{1,0:T(1,128)S(1)} %get-tuple-element.11.c_ref), custom_call_target="tpu_custom_call" | custom-call | tf_op jit(solution)/shard_map/pallas_call | solution.py:608
